TPU v7x, 32 devices: a whole 2x2x4 slice. The times are simulated.
32 devices in a mesh: grp: 2 (over y), row: 4 (over z), col: 2 (over x), half: 2 (over core).
Axes of the slice: x: 2, y: 2, z: 4, core: 2. Of those that a mesh axis runs over, the one named last changes fastest.
Arguments:
- vecs: bfloat16 [4, 1024, 32768], P(('grp', 'half'), 'row', 'col'), parts along dimension 0, may hold values from -6 to 6
- poles: float32 [4, 32768], P(('grp', 'half'), 'col'), parts along dimension 0, may hold values from -512 to 512, as said below
- weights: float32 [4, 32768], P(('grp', 'half'), 'col'), parts along dimension 0, may hold values from -5 to 5
- kept: int32 [4, 32768], P(('grp', 'half'), 'col'), parts along dimension 0, may hold values 0 or 1
- roots: float32 [1024], P(('grp', 'row')), parts along dimension 0, may hold values from -512 to 512, as said below
- order: int32 [1024], P('grp'), parts along dimension 0, may hold values from 0 to 511, each once
Outputs:
- merged: bfloat16 [16, 4, 2, 32, 512], P(('grp', 'row', 'half'), None, None, None, 'col'), parts along dimension 0
There are 2 independent parts, one for each index of `grp`. A program takes and returns all parts, laid end to end along the dimension named above; each array names one. Nothing has to cross between parts.
Inputs may be any that keep to these rules, and one draw needn't show every extreme that they name: `poles`: every root differs from every pole by 0.2 or more. `roots`: every root differs from every pole by 0.2 or more. `order`: A permutation of 0 to 511.
All inputs are finite; a program needn't handle non-finite values. No bound on the sum of `kept` on one device may be relied on, other than what follows from the above.
Results may differ from a plain program's by a relative error of at most 0.0049.
Values may be sent and summed in bfloat16 or wider, within the bound.
A program may use at most 64 MiB of HBM per device.

v0:
```python
import functools

import jax
import jax.numpy as jnp
from jax import lax
from jax.experimental import pallas as pl
from jax.experimental.pallas import tpu as pltpu
from jax.sharding import PartitionSpec as P

MESH = pl.DeviceIdType.MESH
LANES = 128


def kernel(dims, vecs, poles, weights, kept, roots, order, out,
           vbuf, rootbuf, theta, scaled, picks, raw, mask, centers, own, zeven, zodd, acc, nacc, psend, precv, nsend, nrecv, asend, arecv,
           ssem, vsem, rsend, rrecv, pssem, prsem, nssem, nrsem, assem, arsem):
    n_row, n_col, n_half, cols, panel, block, rows = dims
    grp, row, col, half = (lax.axis_index(a) for a in ("grp", "row", "col", "half"))
    share = panel // n_col
    width = panel // n_row
    nrows = vbuf.shape[1]
    groups = n_row * n_half
    depth = nrows // groups
    n_blocks = cols // block

    tiles = block // LANES

    def tile_load(i, j):
        at = pl.ds(pl.multiple_of(i * block + j * LANES, LANES), LANES)
        return pltpu.make_async_copy(vecs.at[0, :, at], vbuf.at[i * tiles + j], vsem.at[i])

    def loaded(i):
        here = vbuf.at[pl.ds(i * tiles, tiles)]
        pltpu.make_async_copy(here, here, vsem.at[i]).wait()

    me = row * n_half + half
    barrier = pltpu.get_barrier_semaphore()
    for o in range(1, groups):
        g = lax.rem(me + o, groups)
        pl.semaphore_signal(barrier, inc=1, device_id=(grp, g // n_half, col, lax.rem(g, n_half)), device_id_type=MESH)
    for t in range(1, n_col):
        for h in range(n_half):
            pl.semaphore_signal(barrier, inc=1, device_id=(grp, row, lax.rem(col + t, n_col), h), device_id_type=MESH)

    small = [(order, picks), (weights, raw), (kept, mask), (poles, centers), (roots, own)]
    fetches = [pltpu.make_async_copy(src, dst, ssem.at[n]) for n, (src, dst) in enumerate(small)]
    for fetch in fetches:
        fetch.start()

    for i in range(n_blocks):
        for j in range(tiles):
            tile_load(i, j).start()
    acc[...] = jnp.zeros_like(acc)
    zodd[...] = jnp.zeros_like(zodd)
    pl.semaphore_wait(barrier, groups - 1 + (n_col - 1) * n_half)

    def root_copy(o):
        return pltpu.make_async_remote_copy(
            src_ref=roots, dst_ref=rootbuf.at[o], send_sem=rsend.at[o], recv_sem=rrecv.at[o],
            device_id=(grp, lax.rem(row + o, n_row), col, half), device_id_type=MESH)

    for o in range(1, n_row):
        root_copy(o).start()
    for fetch in fetches:
        fetch.wait()
    scaled[...] = raw[...] * mask[...].astype(jnp.float32)
    wanted = jnp.transpose(jnp.broadcast_to(picks[...], (LANES, panel)))[:, :width]
    lane = lax.broadcasted_iota(jnp.int32, (panel, width), 1)
    picked = jnp.zeros((panel, width), jnp.float32)
    for o in range(n_row):
        if o:
            root_copy(o).wait()
        source = lax.rem(row + n_row - o, n_row)
        picked = jnp.where(wanted - source * width == lane, rootbuf[o] if o else own[...], picked)
    theta[...] = jnp.broadcast_to(jnp.sum(picked, axis=1, keepdims=True), (panel, LANES))

    strips = share // rows
    span = tiles // strips

    def dot(z, i, k):
        acc[...] += lax.dot_general(
            jnp.concatenate([vbuf[i * tiles + k * span + j] for j in range(span)], axis=1),
            jnp.concatenate([z[k * span + j] for j in range(span)], axis=1),
            (((1,), (1,)), ((), ())), preferred_element_type=jnp.float32)

    def chunk(t):
        base = lax.rem(col + t, n_col) * share
        nacc[...] = jnp.zeros_like(nacc)

        def fill(z, i, k):
            first = pl.multiple_of(k * rows, rows)
            th = [theta[pl.ds(pl.multiple_of(base + k * rows + r, 16), 16), :] for r in range(0, rows, 16)]
            squares = [nacc[pl.ds(first + r, 16), :] for r in range(0, rows, 16)]
            for j in range(tiles):
                at = pl.ds(pl.multiple_of(i * block + j * LANES, LANES), LANES)
                weight, center = scaled[:, at], centers[:, at]
                for n in range(rows // 16):
                    cauchy = weight / (center - th[n])
                    squares[n] += cauchy * cauchy
                    z[j, pl.ds(first + n * 16, 16), :] = cauchy.astype(jnp.bfloat16)
            for n in range(rows // 16):
                nacc[pl.ds(first + n * 16, 16), :] = squares[n]

        def pair(p, carry):
            def even(k, carry):
                dot(zodd, jnp.maximum(2 * p - 1, 0), k)
                fill(zeven, 2 * p, k)
                return carry

            def odd(k, carry):
                dot(zeven, 2 * p, k)
                fill(zodd, 2 * p + 1, k)
                return carry

            if t == 1 or n_col == 1:
                loaded(2 * p)
                loaded(2 * p + 1)
            lax.fori_loop(0, strips, even, 0)

            @pl.when(p == 0)
            def _():
                acc[...] = jnp.zeros_like(acc)

            lax.fori_loop(0, strips, odd, 0)
            return carry

        lax.fori_loop(0, n_blocks // 2, pair, 0)

        def rest(k, carry):
            dot(zodd, n_blocks - 1, k)
            return carry

        lax.fori_loop(0, strips, rest, 0)
        nsend[t] = jnp.sum(jnp.transpose(nacc[...]), axis=0, keepdims=True)

    def norm_copy(t, o):
        return pltpu.make_async_remote_copy(
            src_ref=nsend.at[t], dst_ref=nrecv.at[t, o], send_sem=nssem.at[t, o], recv_sem=nrsem.at[t, o],
            device_id=(grp, row, lax.rem(col + t, n_col), lax.rem(half + o, n_half)), device_id_type=MESH)

    def part_copy(t):
        return pltpu.make_async_remote_copy(
            src_ref=psend.at[t - 1], dst_ref=precv.at[t - 1], send_sem=pssem.at[t - 1], recv_sem=prsem.at[t - 1],
            device_id=(grp, row, lax.rem(col + t, n_col), half), device_id_type=MESH)

    def piece_copy(o):
        g = lax.rem(me + o, groups)
        return pltpu.make_async_remote_copy(
            src_ref=asend.at[g], dst_ref=arecv.at[o], send_sem=assem.at[o], recv_sem=arsem.at[o],
            device_id=(grp, g // n_half, col, lax.rem(g, n_half)), device_id_type=MESH)

    norm_copies = [(t, o) for t in range(n_col) for o in range(n_half) if t or o]
    for t in range(1, n_col):
        chunk(t)
        psend[t - 1] = acc[...].astype(jnp.bfloat16)
        part_copy(t).start()
        for o in range(n_half):
            norm_copy(t, o).start()
    chunk(0)
    for o in range(1, n_half):
        norm_copy(0, o).start()
    total = acc[...]
    for t in range(1, n_col):
        part_copy(t).wait()
        total += precv[t - 1].astype(jnp.float32)
    asend[...] = total.reshape(groups, depth, share).astype(jnp.bfloat16)
    for o in range(1, groups):
        piece_copy(o).start()
    norms = nsend[0]
    for t, o in norm_copies:
        norm_copy(t, o).wait()
        norms += nrecv[t, o]
    scale = lax.rsqrt(norms + 1e-06)
    for o in range(groups):
        if o:
            piece_copy(o).wait()
        g = lax.rem(me + groups - o, groups)
        piece = arecv[o] if o else asend[me]
        out[0, g // n_half, lax.rem(g, n_half)] = (piece.astype(jnp.float32) * scale).astype(jnp.bfloat16)


def body(vecs, poles, weights, kept, roots, order):
    n_row, n_col, n_half = (lax.axis_size(a) for a in ("row", "col", "half"))
    nrows, cols = vecs.shape[1:]
    panel = order.shape[0]
    share, groups = panel // n_col, n_row * n_half
    depth = nrows // groups
    block = min(4096, cols // 2)
    rows = min(128, share)
    vmem = pl.BlockSpec(memory_space=pltpu.VMEM)
    dma = pltpu.SemaphoreType.DMA
    others = max(n_col - 1, 1)
    return pl.pallas_call(
        functools.partial(kernel, (n_row, n_col, n_half, cols, panel, block, rows)),
        out_shape=jax.ShapeDtypeStruct((1, n_row, n_half, depth, share), jnp.bfloat16),
        in_specs=[pl.BlockSpec(memory_space=pl.ANY)] * 6,
        out_specs=vmem,
        scratch_shapes=[
            pltpu.VMEM((cols // LANES, nrows, LANES), jnp.bfloat16),
            pltpu.VMEM((n_row, 1, panel // n_row), jnp.float32),
            pltpu.VMEM((panel, LANES), jnp.float32),
            pltpu.VMEM((1, cols), jnp.float32),
            pltpu.VMEM((1, panel), jnp.int32),
            pltpu.VMEM((1, cols), jnp.float32),
            pltpu.VMEM((1, cols), jnp.int32),
            pltpu.VMEM((1, cols), jnp.float32),
            pltpu.VMEM((1, panel // n_row), jnp.float32),
            pltpu.VMEM((block // LANES, share, LANES), jnp.bfloat16),
            pltpu.VMEM((block // LANES, share, LANES), jnp.bfloat16),
            pltpu.VMEM((nrows, share), jnp.float32),
            pltpu.VMEM((share, LANES), jnp.float32),
            pltpu.VMEM((others, nrows, share), jnp.bfloat16),
            pltpu.VMEM((others, nrows, share), jnp.bfloat16),
            pltpu.VMEM((n_col, 1, share), jnp.float32),
            pltpu.VMEM((n_col, n_half, 1, share), jnp.float32),
            pltpu.VMEM((groups, depth, share), jnp.bfloat16),
            pltpu.VMEM((groups, depth, share), jnp.bfloat16),
            dma((5,)),
            dma((cols // block,)),
            dma((n_row,)),
            dma((n_row,)),
            dma((others,)),
            dma((others,)),
            dma((n_col, n_half)),
            dma((n_col, n_half)),
            dma((groups,)),
            dma((groups,)),
        ],
        compiler_params=pltpu.CompilerParams(collective_id=0, has_side_effects=True),
        name="merge",
    )(vecs, poles, weights, kept, roots[None, :], order[None, :])


def solution(mesh):
    return jax.shard_map(
        body,
        mesh=mesh,
        in_specs=(
            P(("grp", "half"), "row", "col"),
            P(("grp", "half"), "col"),
            P(("grp", "half"), "col"),
            P(("grp", "half"), "col"),
            P(("grp", "row")),
            P("grp"),
        ),
        out_specs=P(("grp", "row", "half"), None, None, None, "col"),
        check_vma=False,
    )
```

profile of v0, /device:TPU:0, one launch (start us, length us, event | category | flops | bytes accessed | tf_op | source)
XLA Modules:
  0.0 25.6 jit_solution(13393913637595145831)
XLA Ops:
  0.0 24.0 %merge.1 = bf16[1,4,2,32,256]{4,3,2,1,0:T(8,128)(2,1)} custom-call(bf16[1,256,16384]{2,1,0:T(8,128)(2,1)} %vecs.1, f32[1,16384]{1,0:T(1,128)} %poles.1, f32[1,16384]{1,0:T(1,128)} %weights.1, s32[1,16384]{1,0:T(1,128)} %kept.1, f32[1,128]{1,0:T(1,128)} %bitcast.3, s32[1,512]{1,0:T(1,128)} %bitcast.2), custom_call_target="tpu_custom_call" | custom-call | tf_op jit(solution)/shard_map/merge/pallas_call | solution.py:193
  24.0 1.6 %copy.8 = bf16[1,4,2,32,256]{4,3,2,1,0:T(8,128)(2,1)} copy(bf16[1,4,2,32,256]{4,3,2,1,0:T(8,128)(2,1)} %merge.1) | data formatting | bytes 262144
where the time goes:
time: 25.7 us; the launch traced here: 25.6 us
  Pallas kernels  24 us (93%)
  local copies, waits for them, and re-layouts  1.57 us (6%)
    pallas_call x1, Pallas kernels, body(): pl.pallas_call(functools.partial(kernel, (n_row, n_col, n_half, cols, pan...  24 us
    unnamed x1, local copies, waits for them, and re-layouts  1.57 us

commit v1 on v0

v1 whole, which is shorter than its diff:
```python
import functools

import jax
import jax.numpy as jnp
from jax import lax
from jax.experimental import pallas as pl
from jax.experimental.pallas import tpu as pltpu
from jax.sharding import PartitionSpec as P

MESH = pl.DeviceIdType.MESH
LANES = 128
PAIRED = 0


def kernel(dims, vecs, poles, weights, kept, roots, order, out,
           vbuf, rootbuf, theta, scaled, picks, raw, mask, centers, own, zeven, zodd, acc, nacc, asend, arecv,
           nsend, nrecv, fsend, frecv,
           ssem, vsem, rsend, rrecv, nssem, nrsem, fssem, frsem, assem, arsem):
    n_row, n_col, n_half, cols, panel, slab = dims
    grp, row, col, half = (lax.axis_index(a) for a in ("grp", "row", "col", "half"))
    share = panel // n_col
    width = panel // n_row
    nrows = vbuf.shape[1]
    groups = n_row * n_half
    depth = nrows // groups
    n_slabs = cols // slab
    tiles = slab // LANES
    me = row * n_half + half

    barrier = pltpu.get_barrier_semaphore()
    for o in range(1, groups):
        g = lax.rem(me + o, groups)
        pl.semaphore_signal(barrier, inc=1, device_id=(grp, g // n_half, col, lax.rem(g, n_half)), device_id_type=MESH)
    for t in range(1, n_col):
        for h in range(n_half):
            pl.semaphore_signal(barrier, inc=1, device_id=(grp, row, lax.rem(col + t, n_col), h), device_id_type=MESH)

    small = [(roots, own), (weights, raw), (kept, mask), (poles, centers), (order, picks)]
    fetches = [pltpu.make_async_copy(src, dst, ssem.at[n]) for n, (src, dst) in enumerate(small)]
    for fetch in fetches:
        fetch.start()

    def fetch_tile(n, carry):
        at = pl.ds(pl.multiple_of(n * LANES, LANES), LANES)
        pltpu.make_async_copy(vecs.at[0, :, at], vbuf.at[n], vsem.at[n // tiles]).start()
        return carry

    def loaded(i):
        here = vbuf.at[pl.ds(i * tiles, tiles)]
        pltpu.make_async_copy(here, here, vsem.at[i]).wait()

    lax.fori_loop(0, n_slabs * tiles, fetch_tile, 0)
    acc[...] = jnp.zeros_like(acc)
    zodd[...] = jnp.zeros_like(zodd)
    pl.semaphore_wait(barrier, groups - 1 + (n_col - 1) * n_half)

    def root_copy(o, h):
        return pltpu.make_async_remote_copy(
            src_ref=roots, dst_ref=rootbuf.at[o], send_sem=rsend.at[o, h], recv_sem=rrecv.at[o],
            device_id=(grp, lax.rem(row + o, n_row), col, h), device_id_type=MESH)

    @pl.when(half == n_half - 1)
    def _():
        for o in range(1, n_row):
            for h in range(n_half):
                root_copy(o, h).start()

    for fetch in fetches:
        fetch.wait()
    scaled[...] = raw[...] * mask[...].astype(jnp.float32)
    nacc[...] = jnp.zeros_like(nacc)
    span = min(width, 128)

    for first in range(0, width, span):
        mine = [jnp.transpose(jnp.broadcast_to(own[:, first:first + span], (LANES, span)))[r:r + 8] for r in range(0, span, 8)]

        def norm_step(i, squares):
            for j in range(4):
                at = pl.ds(pl.multiple_of(i * 4 * LANES + j * LANES, LANES), LANES)
                weight, center = scaled[:, at], centers[:, at]
                cauchy = [weight / (center - m) for m in mine]
                squares = [s + c * c for s, c in zip(squares, cauchy)]
            return squares

        squares = lax.fori_loop(0, cols // (4 * LANES), norm_step, [jnp.zeros((8, LANES), jnp.float32) for _ in mine])
        for n, s in enumerate(squares):
            nacc[pl.ds(first + n * 8, 8), :] = s
    nsend[...] = jnp.sum(jnp.transpose(nacc[...]), axis=0, keepdims=True)

    def norm_copy(t, o):
        return pltpu.make_async_remote_copy(
            src_ref=nsend, dst_ref=nrecv.at[t, o], send_sem=nssem.at[t, o], recv_sem=nrsem.at[t, o],
            device_id=(grp, row, lax.rem(col + t, n_col), lax.rem(half + o, n_half)), device_id_type=MESH)

    norm_copies = [(t, o) for t in range(n_col) for o in range(n_half) if t or o]
    for t, o in norm_copies:
        norm_copy(t, o).start()

    wanted = jnp.transpose(jnp.broadcast_to(picks[...], (LANES, panel)))[:, :width]
    lane = lax.broadcasted_iota(jnp.int32, (panel, width), 1)
    picked = jnp.zeros((panel, width), jnp.float32)
    for o in range(n_row):
        if o:
            root_copy(o, 0).wait_recv()
        source = lax.rem(row + n_row - o, n_row)
        picked = jnp.where(wanted - source * width == lane, rootbuf[o] if o else own[...], picked)
    theta[...] = jnp.broadcast_to(jnp.sum(picked, axis=1, keepdims=True), (panel, LANES))

    def dot(z, i, k):
        acc[...] += lax.dot_general(
            jnp.concatenate([vbuf[(i * 2 + k) * tiles + j] for j in range(tiles)], axis=1),
            jnp.concatenate([z[k * tiles + j] for j in range(tiles)], axis=1),
            (((1,), (1,)), ((), ())), preferred_element_type=jnp.float32)

    def piece_copy(t, o):
        g = lax.rem(me + o, groups)
        return pltpu.make_async_remote_copy(
            src_ref=asend.at[t, g], dst_ref=arecv.at[t, o], send_sem=assem.at[t, o], recv_sem=arsem.at[t, o],
            device_id=(grp, g // n_half, lax.rem(col + t, n_col), lax.rem(g, n_half)), device_id_type=MESH)

    def flush(t):
        asend[t] = acc[...].reshape(groups, depth, share).astype(jnp.bfloat16)
        for o in range(0 if t else 1, groups):
            piece_copy(t, o).start()

    def chunk(t, last):
        base = lax.rem(col + t, n_col) * share

        def fill(z, i, k):
            thetas = [theta[pl.ds(pl.multiple_of(base + r, 16), 16), :] for r in range(0, share, 16)]
            for j in range(tiles):
                at = pl.ds(pl.multiple_of((i * 2 + k) * slab + j * LANES, LANES), LANES)
                weight, center = scaled[:, at], centers[:, at]
                for n in range(0, share // 16, 2):
                    a, b = (center - th for th in thetas[n:n + 2])
                    if (n // 2) % 4 < PAIRED:
                        both = weight / (a * b)
                        left, right = both * b, both * a
                    else:
                        left, right = weight / a, weight / b
                    z[k * tiles + j, pl.ds(n * 16, 16), :] = left.astype(jnp.bfloat16)
                    z[k * tiles + j, pl.ds(n * 16 + 16, 16), :] = right.astype(jnp.bfloat16)

        def pair(p, carry):
            if last is None:
                for n in range(4):
                    loaded(4 * p + n)
            before = jnp.where(p == 0, 0 if last is None else n_slabs // 2 - 1, 2 * p - 1)

            def even(k, carry):
                dot(zodd, before, k)
                fill(zeven, 2 * p, k)
                return carry

            def odd(k, carry):
                dot(zeven, 2 * p, k)
                fill(zodd, 2 * p + 1, k)
                return carry

            lax.fori_loop(0, 2, even, 0)

            @pl.when(p == 0)
            def _():
                if last is not None:
                    flush(last)
                acc[...] = jnp.zeros_like(acc)

            lax.fori_loop(0, 2, odd, 0)
            return carry

        lax.fori_loop(0, n_slabs // 4, pair, 0)

    last = None
    for t in [*range(1, n_col), 0]:
        chunk(t, last)
        if last is None:
            total = nsend[...]
            for pair in norm_copies:
                norm_copy(*pair).wait()
                total += nrecv[pair]
            fsend[...] = lax.rsqrt(total + 1e-06)

            def factor_copy(o):
                return pltpu.make_async_remote_copy(
                    src_ref=fsend, dst_ref=frecv.at[o], send_sem=fssem.at[o], recv_sem=frsem.at[o],
                    device_id=(grp, lax.rem(row + o, n_row), col, half), device_id_type=MESH)

            for o in range(1, n_row):
                factor_copy(o).start()
        last = t

    def rest(k, carry):
        dot(zodd, n_slabs // 2 - 1, k)
        return carry

    lax.fori_loop(0, 2, rest, 0)
    flush(0)

    chosen = picks[:, pl.ds(pl.multiple_of(col * share, LANES), share)]
    index = lax.broadcasted_iota(jnp.int32, (width, share), 0)
    scale = jnp.zeros((width, share), jnp.float32)
    for o in range(n_row):
        if o:
            factor_copy(o).wait()
        source = lax.rem(row + n_row - o, n_row)
        factor = frecv[o] if o else fsend[...]
        column = jnp.transpose(jnp.broadcast_to(factor, (LANES, width)))[:, :1]
        scale = jnp.where(chosen - source * width == index, column, scale)
    scale = jnp.sum(scale, axis=0, keepdims=True)

    @pl.when(half == n_half - 1)
    def _():
        for o in range(1, n_row):
            for h in range(n_half):
                root_copy(o, h).wait_send()

    for o in range(groups):
        g = lax.rem(me + groups - o, groups)
        piece = jnp.zeros((depth, share), jnp.float32)
        for t in [*range(1, n_col), 0]:
            if t or o:
                piece_copy(t, o).wait()
            piece += (arecv[t, o] if t or o else asend[0, me]).astype(jnp.float32)
        out[0, g // n_half, lax.rem(g, n_half)] = (piece * scale).astype(jnp.bfloat16)


def body(vecs, poles, weights, kept, roots, order):
    n_row, n_col, n_half = (lax.axis_size(a) for a in ("row", "col", "half"))
    nrows, cols = vecs.shape[1:]
    panel = order.shape[0]
    share, groups, width = panel // n_col, n_row * n_half, panel // n_row
    depth = nrows // groups
    slab = min(2048, cols // 4)
    dma = pltpu.SemaphoreType.DMA
    return pl.pallas_call(
        functools.partial(kernel, (n_row, n_col, n_half, cols, panel, slab)),
        out_shape=pltpu.VMEM((1, n_row, n_half, depth, share), jnp.bfloat16),
        in_specs=[pl.BlockSpec(memory_space=pl.ANY)] * 6,
        out_specs=pl.BlockSpec(memory_space=pltpu.VMEM),
        scratch_shapes=[
            pltpu.VMEM((cols // LANES, nrows, LANES), jnp.bfloat16),
            pltpu.VMEM((n_row, 1, width), jnp.float32),
            pltpu.VMEM((panel, LANES), jnp.float32),
            pltpu.VMEM((1, cols), jnp.float32),
            pltpu.VMEM((1, panel), jnp.int32),
            pltpu.VMEM((1, cols), jnp.float32),
            pltpu.VMEM((1, cols), jnp.int32),
            pltpu.VMEM((1, cols), jnp.float32),
            pltpu.VMEM((1, width), jnp.float32),
            pltpu.VMEM((2 * slab // LANES, share, LANES), jnp.bfloat16),
            pltpu.VMEM((2 * slab // LANES, share, LANES), jnp.bfloat16),
            pltpu.VMEM((nrows, share), jnp.float32),
            pltpu.VMEM((width, LANES), jnp.float32),
            pltpu.VMEM((n_col, groups, depth, share), jnp.bfloat16),
            pltpu.VMEM((n_col, groups, depth, share), jnp.bfloat16),
            pltpu.VMEM((1, width), jnp.float32),
            pltpu.VMEM((n_col, n_half, 1, width), jnp.float32),
            pltpu.VMEM((1, width), jnp.float32),
            pltpu.VMEM((n_row, 1, width), jnp.float32),
            dma((5,)),
            dma((cols // slab,)),
            dma((n_row, n_half)),
            dma((n_row,)),
            dma((n_col, n_half)),
            dma((n_col, n_half)),
            dma((n_row,)),
            dma((n_row,)),
            dma((n_col, groups)),
            dma((n_col, groups)),
        ],
        compiler_params=pltpu.CompilerParams(collective_id=0, has_side_effects=True),
        name="merge",
    )(vecs, poles, weights, kept, roots[None, :], order[None, :])


def solution(mesh):
    return jax.shard_map(
        body,
        mesh=mesh,
        in_specs=(
            P(("grp", "half"), "row", "col"),
            P(("grp", "half"), "col"),
            P(("grp", "half"), "col"),
            P(("grp", "half"), "col"),
            P(("grp", "row")),
            P("grp"),
        ),
        out_specs=P(("grp", "row", "half"), None, None, None, "col"),
        check_vma=False,
    )
```

time: 25.7 us -> 23.3 us (0.907)
  Pallas kernels: 24 us -> 22.4 us
  local copies, waits for them, and re-layouts: 1.57 us -> 0.66 us
    pallas_call x1, Pallas kernels: 24 us -> 22.4 us  [body(): pl.pallas_call(functools.partial(kernel, (n_row, n_col, n_half, cols, pan...]
    unnamed x1, local copies, waits for them, and re-layouts: 1.57 us -> 0.66 us
where the time goes in v1:
time: 23.3 us; the launch traced here: 23.1 us
  Pallas kernels  22.4 us (96%)
  local copies, waits for them, and re-layouts  0.66 us (3%)
    pallas_call x1, Pallas kernels, body(): pl.pallas_call(functools.partial(kernel, (n_row, n_col, n_half, cols, pan...  22.4 us
    unnamed x1, local copies, waits for them, and re-layouts  0.66 us

profile of v1, /device:TPU:0, one launch (start us, length us, event | category | flops | bytes accessed | tf_op | source)
XLA Modules:
  0.0 23.1 jit_solution(16897629034694871158)
XLA Ops:
  0.0 22.4 %merge.1 = bf16[1,4,2,32,256]{4,3,2,1,0:T(8,128)(2,1)S(1)} custom-call(bf16[1,256,16384]{2,1,0:T(8,128)(2,1)} %vecs.1, f32[1,16384]{1,0:T(1,128)} %poles.1, f32[1,16384]{1,0:T(1,128)} %weights.1, s32[1,16384]{1,0:T(1,128)} %kept.1, f32[1,128]{1,0:T(1,128)} %bitcast.3, s32[1,512]{1,0:T(1,128)} %bitcast.2), custom_call_target="tpu_custom_call" | custom-call | tf_op jit(solution)/shard_map/merge/pallas_call | solution.py:235
  22.5 0.7 %copy.8 = bf16[1,4,2,32,256]{4,3,2,1,0:T(8,128)(2,1)} copy(bf16[1,4,2,32,256]{4,3,2,1,0:T(8,128)(2,1)S(1)} %merge.1) | data formatting | bytes 262144

commit v2 on v1

--- a/solution.py
+++ b/solution.py
@@ -9,11 +9,12 @@
 
 MESH = pl.DeviceIdType.MESH
 LANES = 128
-PAIRED = 0
+PAIRED = 1
+SLAB = 8192
 
 
 def kernel(dims, vecs, poles, weights, kept, roots, order, out,
-           vbuf, rootbuf, theta, scaled, picks, raw, mask, centers, own, zeven, zodd, acc, nacc, asend, arecv,
+           vbuf, rootbuf, theta, scaled, picks, raw, mask, centers, own, z, acc, nacc, asend, arecv,
            nsend, nrecv, fsend, frecv,
            ssem, vsem, rsend, rrecv, nssem, nrsem, fssem, frsem, assem, arsem):
     n_row, n_col, n_half, cols, panel, slab = dims
@@ -50,8 +51,6 @@
         pltpu.make_async_copy(here, here, vsem.at[i]).wait()
 
     lax.fori_loop(0, n_slabs * tiles, fetch_tile, 0)
-    acc[...] = jnp.zeros_like(acc)
-    zodd[...] = jnp.zeros_like(zodd)
     pl.semaphore_wait(barrier, groups - 1 + (n_col - 1) * n_half)
 
     def root_copy(o, h):
@@ -106,12 +105,6 @@
         picked = jnp.where(wanted - source * width == lane, rootbuf[o] if o else own[...], picked)
     theta[...] = jnp.broadcast_to(jnp.sum(picked, axis=1, keepdims=True), (panel, LANES))
 
-    def dot(z, i, k):
-        acc[...] += lax.dot_general(
-            jnp.concatenate([vbuf[(i * 2 + k) * tiles + j] for j in range(tiles)], axis=1),
-            jnp.concatenate([z[k * tiles + j] for j in range(tiles)], axis=1),
-            (((1,), (1,)), ((), ())), preferred_element_type=jnp.float32)
-
     def piece_copy(t, o):
         g = lax.rem(me + o, groups)
         return pltpu.make_async_remote_copy(
@@ -123,57 +116,42 @@
         for o in range(0 if t else 1, groups):
             piece_copy(t, o).start()
 
-    def chunk(t, last):
+    def chunk(t):
         base = lax.rem(col + t, n_col) * share
-
-        def fill(z, i, k):
+        acc[...] = jnp.zeros_like(acc)
+
+        def step(i, carry):
+            if t == 1 or n_col == 1:
+                loaded(i)
             thetas = [theta[pl.ds(pl.multiple_of(base + r, 16), 16), :] for r in range(0, share, 16)]
-            for j in range(tiles):
-                at = pl.ds(pl.multiple_of((i * 2 + k) * slab + j * LANES, LANES), LANES)
-                weight, center = scaled[:, at], centers[:, at]
-                for n in range(0, share // 16, 2):
-                    a, b = (center - th for th in thetas[n:n + 2])
-                    if (n // 2) % 4 < PAIRED:
-                        both = weight / (a * b)
-                        left, right = both * b, both * a
-                    else:
-                        left, right = weight / a, weight / b
-                    z[k * tiles + j, pl.ds(n * 16, 16), :] = left.astype(jnp.bfloat16)
-                    z[k * tiles + j, pl.ds(n * 16 + 16, 16), :] = right.astype(jnp.bfloat16)
-
-        def pair(p, carry):
-            if last is None:
-                for n in range(4):
-                    loaded(4 * p + n)
-            before = jnp.where(p == 0, 0 if last is None else n_slabs // 2 - 1, 2 * p - 1)
-
-            def even(k, carry):
-                dot(zodd, before, k)
-                fill(zeven, 2 * p, k)
-                return carry
-
-            def odd(k, carry):
-                dot(zeven, 2 * p, k)
-                fill(zodd, 2 * p + 1, k)
-                return carry
-
-            lax.fori_loop(0, 2, even, 0)
-
-            @pl.when(p == 0)
-            def _():
-                if last is not None:
-                    flush(last)
-                acc[...] = jnp.zeros_like(acc)
-
-            lax.fori_loop(0, 2, odd, 0)
+            sums = [None, None]
+            for m in range(tiles // 2):
+                for j in (2 * m, 2 * m + 1):
+                    at = pl.ds(pl.multiple_of(i * slab + j * LANES, LANES), LANES)
+                    weight, center = scaled[:, at], centers[:, at]
+                    for n in range(0, share // 16, 2):
+                        a, b = (center - th for th in thetas[n:n + 2])
+                        if (n // 2) % 4 < PAIRED:
+                            both = weight / (a * b)
+                            left, right = both * b, both * a
+                        else:
+                            left, right = weight / a, weight / b
+                        z[j, pl.ds(n * 16, 16), :] = left.astype(jnp.bfloat16)
+                        z[j, pl.ds(n * 16 + 16, 16), :] = right.astype(jnp.bfloat16)
+                part = lax.dot_general(
+                    jnp.concatenate([vbuf[i * tiles + j] for j in (2 * m, 2 * m + 1)], axis=1),
+                    jnp.concatenate([z[j] for j in (2 * m, 2 * m + 1)], axis=1),
+                    (((1,), (1,)), ((), ())), preferred_element_type=jnp.float32)
+                sums[m % 2] = part if sums[m % 2] is None else sums[m % 2] + part
+            acc[...] += sums[0] + sums[1]
             return carry
 
-        lax.fori_loop(0, n_slabs // 4, pair, 0)
-
-    last = None
+        lax.fori_loop(0, n_slabs, step, 0)
+
     for t in [*range(1, n_col), 0]:
-        chunk(t, last)
-        if last is None:
+        chunk(t)
+        flush(t)
+        if t == 1 or n_col == 1:
             total = nsend[...]
             for pair in norm_copies:
                 norm_copy(*pair).wait()
@@ -187,14 +165,6 @@
 
             for o in range(1, n_row):
                 factor_copy(o).start()
-        last = t
-
-    def rest(k, carry):
-        dot(zodd, n_slabs // 2 - 1, k)
-        return carry
-
-    lax.fori_loop(0, 2, rest, 0)
-    flush(0)
 
     chosen = picks[:, pl.ds(pl.multiple_of(col * share, LANES), share)]
     index = lax.broadcasted_iota(jnp.int32, (width, share), 0)
@@ -230,7 +200,7 @@
     panel = order.shape[0]
     share, groups, width = panel // n_col, n_row * n_half, panel // n_row
     depth = nrows // groups
-    slab = min(2048, cols // 4)
+    slab = min(SLAB, cols)
     dma = pltpu.SemaphoreType.DMA
     return pl.pallas_call(
         functools.partial(kernel, (n_row, n_col, n_half, cols, panel, slab)),
@@ -247,8 +217,7 @@
             pltpu.VMEM((1, cols), jnp.int32),
             pltpu.VMEM((1, cols), jnp.float32),
             pltpu.VMEM((1, width), jnp.float32),
-            pltpu.VMEM((2 * slab // LANES, share, LANES), jnp.bfloat16),
-            pltpu.VMEM((2 * slab // LANES, share, LANES), jnp.bfloat16),
+            pltpu.VMEM((slab // LANES, share, LANES), jnp.bfloat16),
             pltpu.VMEM((nrows, share), jnp.float32),
             pltpu.VMEM((width, LANES), jnp.float32),
             pltpu.VMEM((n_col, groups, depth, share), jnp.bfloat16),

time: 23.3 us -> 20.1 us (0.86)
  Pallas kernels: 22.4 us -> 19.3 us
    pallas_call x1, Pallas kernels: 22.4 us -> 19.3 us  [body(): pl.pallas_call(functools.partial(kernel, (n_row, n_col, n_half, cols, pan...]
where the time goes in v2:
time: 20.1 us; the launch traced here: 19.9 us
  Pallas kernels  19.3 us (96%)
  local copies, waits for them, and re-layouts  0.66 us (3%)
    pallas_call x1, Pallas kernels, body(): pl.pallas_call(functools.partial(kernel, (n_row, n_col, n_half, cols, pan...  19.3 us
    unnamed x1, local copies, waits for them, and re-layouts  0.66 us

profile of v2, /device:TPU:0, one launch (start us, length us, event | category | flops | bytes accessed | tf_op | source)
XLA Modules:
  0.0 19.9 jit_solution(11690967328521395168)
XLA Ops:
  0.0 19.3 %merge.1 = bf16[1,4,2,32,256]{4,3,2,1,0:T(8,128)(2,1)S(1)} custom-call(bf16[1,256,16384]{2,1,0:T(8,128)(2,1)} %vecs.1, f32[1,16384]{1,0:T(1,128)} %poles.1, f32[1,16384]{1,0:T(1,128)} %weights.1, s32[1,16384]{1,0:T(1,128)} %kept.1, f32[1,128]{1,0:T(1,128)} %bitcast.3, s32[1,512]{1,0:T(1,128)} %bitcast.2), custom_call_target="tpu_custom_call" | custom-call | tf_op jit(solution)/shard_map/merge/pallas_call | solution.py:205
  19.3 0.7 %copy.8 = bf16[1,4,2,32,256]{4,3,2,1,0:T(8,128)(2,1)} copy(bf16[1,4,2,32,256]{4,3,2,1,0:T(8,128)(2,1)S(1)} %merge.1) | data formatting | bytes 262144

commit v3 on v2

--- a/solution.py
+++ b/solution.py
@@ -14,7 +14,7 @@
 
 
 def kernel(dims, vecs, poles, weights, kept, roots, order, out,
-           vbuf, rootbuf, theta, scaled, picks, raw, mask, centers, own, z, acc, nacc, asend, arecv,
+           vbuf, rootbuf, theta, scaled, picks, raw, mask, centers, own, acc, nacc, asend, arecv,
            nsend, nrecv, fsend, frecv,
            ssem, vsem, rsend, rrecv, nssem, nrsem, fssem, frsem, assem, arsem):
     n_row, n_col, n_half, cols, panel, slab = dims
@@ -116,40 +116,54 @@
         for o in range(0 if t else 1, groups):
             piece_copy(t, o).start()
 
-    def chunk(t):
+    def columns(i, js, thetas):
+        ats = [pl.ds(pl.multiple_of(i * slab + j * LANES, LANES), LANES) for j in js]
+        rows = [[] for _ in js]
+        for n in range(0, share // 16, 2):
+            for at, parts in zip(ats, rows):
+                weight, center = scaled[:, at], centers[:, at]
+                a, b = (center - th for th in thetas[n:n + 2])
+                if (n // 2) % 4 < PAIRED:
+                    both = weight / (a * b)
+                    left, right = both * b, both * a
+                else:
+                    left, right = weight / a, weight / b
+                parts += [left.astype(jnp.bfloat16), right.astype(jnp.bfloat16)]
+        return jnp.concatenate([jnp.concatenate(parts, axis=0) for parts in rows], axis=1)
+
+    direct = False
+
+    def chunk(t, *accs):
         base = lax.rem(col + t, n_col) * share
-        acc[...] = jnp.zeros_like(acc)
-
-        def step(i, carry):
+
+        def step(i, sums):
             if t == 1 or n_col == 1:
                 loaded(i)
             thetas = [theta[pl.ds(pl.multiple_of(base + r, 16), 16), :] for r in range(0, share, 16)]
-            sums = [None, None]
+            both = [None, None]
             for m in range(tiles // 2):
-                for j in (2 * m, 2 * m + 1):
-                    at = pl.ds(pl.multiple_of(i * slab + j * LANES, LANES), LANES)
-                    weight, center = scaled[:, at], centers[:, at]
-                    for n in range(0, share // 16, 2):
-                        a, b = (center - th for th in thetas[n:n + 2])
-                        if (n // 2) % 4 < PAIRED:
-                            both = weight / (a * b)
-                            left, right = both * b, both * a
-                        else:
-                            left, right = weight / a, weight / b
-                        z[j, pl.ds(n * 16, 16), :] = left.astype(jnp.bfloat16)
-                        z[j, pl.ds(n * 16 + 16, 16), :] = right.astype(jnp.bfloat16)
-                part = lax.dot_general(
-                    jnp.concatenate([vbuf[i * tiles + j] for j in (2 * m, 2 * m + 1)], axis=1),
-                    jnp.concatenate([z[j] for j in (2 * m, 2 * m + 1)], axis=1),
-                    (((1,), (1,)), ((), ())), preferred_element_type=jnp.float32)
-                sums[m % 2] = part if sums[m % 2] is None else sums[m % 2] + part
-            acc[...] += sums[0] + sums[1]
-            return carry
-
+                left = jnp.concatenate([vbuf[i * tiles + j] for j in (2 * m, 2 * m + 1)], axis=1)
+                right = columns(i, (2 * m, 2 * m + 1), thetas)
+                if direct:
+                    pltpu.matmul_push_rhs(right, m // 2 % 2, m % 2, transpose=True)
+                    pltpu.matmul_acc_lhs(accs[m % 2], left, load_staged_rhs=m // 2 % 2)
+                else:
+                    part = lax.dot_general(left, right, (((1,), (1,)), ((), ())), preferred_element_type=jnp.float32)
+                    both[m % 2] = part if both[m % 2] is None else both[m % 2] + part
+            acc[...] += both[0] + both[1]
+            return sums
+
+        acc[...] = jnp.zeros_like(acc)
         lax.fori_loop(0, n_slabs, step, 0)
 
+    def run(t):
+        if direct:
+            pl.run_scoped(functools.partial(chunk, t), *(pltpu.ACC(n)((nrows, share), jnp.float32) for n in range(2)))
+        else:
+            chunk(t)
+
     for t in [*range(1, n_col), 0]:
-        chunk(t)
+        run(t)
         flush(t)
         if t == 1 or n_col == 1:
             total = nsend[...]
@@ -217,7 +231,6 @@
             pltpu.VMEM((1, cols), jnp.int32),
             pltpu.VMEM((1, cols), jnp.float32),
             pltpu.VMEM((1, width), jnp.float32),
-            pltpu.VMEM((slab // LANES, share, LANES), jnp.bfloat16),
             pltpu.VMEM((nrows, share), jnp.float32),
             pltpu.VMEM((width, LANES), jnp.float32),
             pltpu.VMEM((n_col, groups, depth, share), jnp.bfloat16),

time: 20.1 us -> 19.1 us (0.950)
  Pallas kernels: 19.3 us -> 18.3 us
    pallas_call x1, Pallas kernels: 19.3 us -> 18.3 us  [body(): pl.pallas_call(functools.partial(kernel, (n_row, n_col, n_half, cols, pan...]
where the time goes in v3:
time: 19.1 us; the launch traced here: 19 us
  Pallas kernels  18.3 us (96%)
  local copies, waits for them, and re-layouts  0.66 us (3%)
    pallas_call x1, Pallas kernels, body(): pl.pallas_call(functools.partial(kernel, (n_row, n_col, n_half, cols, pan...  18.3 us
    unnamed x1, local copies, waits for them, and re-layouts  0.66 us

profile of v3, /device:TPU:0, one launch (start us, length us, event | category | flops | bytes accessed | tf_op | source)
XLA Modules:
  0.0 19.0 jit_solution(10286064311444219792)
XLA Ops:
  0.0 18.3 %merge.1 = bf16[1,4,2,32,256]{4,3,2,1,0:T(8,128)(2,1)S(1)} custom-call(bf16[1,256,16384]{2,1,0:T(8,128)(2,1)} %vecs.1, f32[1,16384]{1,0:T(1,128)} %poles.1, f32[1,16384]{1,0:T(1,128)} %weights.1, s32[1,16384]{1,0:T(1,128)} %kept.1, f32[1,128]{1,0:T(1,128)} %bitcast.3, s32[1,512]{1,0:T(1,128)} %bitcast.2), custom_call_target="tpu_custom_call" | custom-call | tf_op jit(solution)/shard_map/merge/pallas_call | solution.py:219
  18.3 0.7 %copy.8 = bf16[1,4,2,32,256]{4,3,2,1,0:T(8,128)(2,1)} copy(bf16[1,4,2,32,256]{4,3,2,1,0:T(8,128)(2,1)S(1)} %merge.1) | data formatting | bytes 262144

commit v4 on v3

--- a/solution.py
+++ b/solution.py
@@ -10,7 +10,7 @@
 MESH = pl.DeviceIdType.MESH
 LANES = 128
 PAIRED = 1
-SLAB = 8192
+SLAB = 16384
 
 
 def kernel(dims, vecs, poles, weights, kept, roots, order, out,
@@ -60,7 +60,7 @@
 
     @pl.when(half == n_half - 1)
     def _():
-        for o in range(1, n_row):
+        for o in range(n_row - 1, 0, -1):
             for h in range(n_half):
                 root_copy(o, h).start()
 
@@ -113,8 +113,13 @@
 
     def flush(t):
         asend[t] = acc[...].reshape(groups, depth, share).astype(jnp.bfloat16)
-        for o in range(0 if t else 1, groups):
+
+        for o in range(1, groups):
             piece_copy(t, o).start()
+
+        @pl.when(t > 0)
+        def _():
+            piece_copy(t, 0).start()
 
     def columns(i, js, thetas):
         ats = [pl.ds(pl.multiple_of(i * slab + j * LANES, LANES), LANES) for j in js]
@@ -131,54 +136,48 @@
                 parts += [left.astype(jnp.bfloat16), right.astype(jnp.bfloat16)]
         return jnp.concatenate([jnp.concatenate(parts, axis=0) for parts in rows], axis=1)
 
-    direct = False
-
-    def chunk(t, *accs):
+    def factor_copy(o):
+        return pltpu.make_async_remote_copy(
+            src_ref=fsend, dst_ref=frecv.at[o], send_sem=fssem.at[o], recv_sem=frsem.at[o],
+            device_id=(grp, lax.rem(row + o, n_row), col, half), device_id_type=MESH)
+
+    def chunk(c, carry):
+        t = lax.rem(c + 1, n_col)
         base = lax.rem(col + t, n_col) * share
-
-        def step(i, sums):
-            if t == 1 or n_col == 1:
+        def step(i, carry):
+            @pl.when(c == 0)
+            def _():
                 loaded(i)
+
             thetas = [theta[pl.ds(pl.multiple_of(base + r, 16), 16), :] for r in range(0, share, 16)]
-            both = [None, None]
+            sums = [None, None]
             for m in range(tiles // 2):
                 left = jnp.concatenate([vbuf[i * tiles + j] for j in (2 * m, 2 * m + 1)], axis=1)
                 right = columns(i, (2 * m, 2 * m + 1), thetas)
-                if direct:
-                    pltpu.matmul_push_rhs(right, m // 2 % 2, m % 2, transpose=True)
-                    pltpu.matmul_acc_lhs(accs[m % 2], left, load_staged_rhs=m // 2 % 2)
-                else:
-                    part = lax.dot_general(left, right, (((1,), (1,)), ((), ())), preferred_element_type=jnp.float32)
-                    both[m % 2] = part if both[m % 2] is None else both[m % 2] + part
-            acc[...] += both[0] + both[1]
-            return sums
-
-        acc[...] = jnp.zeros_like(acc)
+                part = lax.dot_general(left, right, (((1,), (1,)), ((), ())), preferred_element_type=jnp.float32)
+                sums[m % 2] = part if sums[m % 2] is None else sums[m % 2] + part
+            if n_slabs == 1:
+                acc[...] = sums[0] + sums[1]
+            else:
+                acc[...] = jnp.where(i == 0, 0.0, acc[...]) + sums[0] + sums[1]
+            return carry
+
         lax.fori_loop(0, n_slabs, step, 0)
-
-    def run(t):
-        if direct:
-            pl.run_scoped(functools.partial(chunk, t), *(pltpu.ACC(n)((nrows, share), jnp.float32) for n in range(2)))
-        else:
-            chunk(t)
-
-    for t in [*range(1, n_col), 0]:
-        run(t)
         flush(t)
-        if t == 1 or n_col == 1:
+
+        @pl.when(c == 0)
+        def _():
             total = nsend[...]
             for pair in norm_copies:
                 norm_copy(*pair).wait()
                 total += nrecv[pair]
             fsend[...] = lax.rsqrt(total + 1e-06)
-
-            def factor_copy(o):
-                return pltpu.make_async_remote_copy(
-                    src_ref=fsend, dst_ref=frecv.at[o], send_sem=fssem.at[o], recv_sem=frsem.at[o],
-                    device_id=(grp, lax.rem(row + o, n_row), col, half), device_id_type=MESH)
-
             for o in range(1, n_row):
                 factor_copy(o).start()
+
+        return carry
+
+    lax.fori_loop(0, n_col, chunk, 0)
 
     chosen = picks[:, pl.ds(pl.multiple_of(col * share, LANES), share)]
     index = lax.broadcasted_iota(jnp.int32, (width, share), 0)

time: 19.1 us -> 18.6 us (0.974)
  Pallas kernels: 18.3 us -> 17.7 us
    pallas_call x1, Pallas kernels: 18.3 us -> 17.7 us  [body(): pl.pallas_call(functools.partial(kernel, (n_row, n_col, n_half, cols, pan...]
where the time goes in v4:
time: 18.6 us; the launch traced here: 18.4 us
  Pallas kernels  17.7 us (95%)
  local copies, waits for them, and re-layouts  0.66 us (4%)
    pallas_call x1, Pallas kernels, body(): pl.pallas_call(functools.partial(kernel, (n_row, n_col, n_half, cols, pan...  17.7 us
    unnamed x1, local copies, waits for them, and re-layouts  0.66 us

profile of v4, /device:TPU:0, one launch (start us, length us, event | category | flops | bytes accessed | tf_op | source)
XLA Modules:
  0.0 18.4 jit_solution(2112746105684479041)
XLA Ops:
  0.0 17.7 %merge.1 = bf16[1,4,2,32,256]{4,3,2,1,0:T(8,128)(2,1)S(1)} custom-call(bf16[1,256,16384]{2,1,0:T(8,128)(2,1)} %vecs.1, f32[1,16384]{1,0:T(1,128)} %poles.1, f32[1,16384]{1,0:T(1,128)} %weights.1, s32[1,16384]{1,0:T(1,128)} %kept.1, f32[1,128]{1,0:T(1,128)} %bitcast.3, s32[1,512]{1,0:T(1,128)} %bitcast.2), custom_call_target="tpu_custom_call" | custom-call | tf_op jit(solution)/shard_map/merge/pallas_call | solution.py:218
  17.7 0.7 %copy.8 = bf16[1,4,2,32,256]{4,3,2,1,0:T(8,128)(2,1)} copy(bf16[1,4,2,32,256]{4,3,2,1,0:T(8,128)(2,1)S(1)} %merge.1) | data formatting | bytes 262144

commit v5 on v4

--- a/solution.py
+++ b/solution.py
@@ -142,7 +142,7 @@
             device_id=(grp, lax.rem(row + o, n_row), col, half), device_id_type=MESH)
 
     def chunk(c, carry):
-        t = lax.rem(c + 1, n_col)
+        t = lax.rem(c + n_col - col, n_col)
         base = lax.rem(col + t, n_col) * share
         def step(i, carry):
             @pl.when(c == 0)

time: 18.6 us -> 17.8 us (0.957)
  Pallas kernels: 17.7 us -> 16.8 us
    pallas_call x1, Pallas kernels: 17.7 us -> 16.8 us  [body(): pl.pallas_call(functools.partial(kernel, (n_row, n_col, n_half, cols, pan...]
where the time goes in v5:
time: 17.8 us; the launch traced here: 17.5 us
  Pallas kernels  16.8 us (94%)
  local copies, waits for them, and re-layouts  0.66 us (4%)
    pallas_call x1, Pallas kernels, body(): pl.pallas_call(functools.partial(kernel, (n_row, n_col, n_half, cols, pan...  16.8 us
    unnamed x1, local copies, waits for them, and re-layouts  0.66 us

profile of v5, /device:TPU:0, one launch (start us, length us, event | category | flops | bytes accessed | tf_op | source)
XLA Modules:
  0.0 17.5 jit_solution(10439435121452124525)
XLA Ops:
  0.0 16.8 %merge.1 = bf16[1,4,2,32,256]{4,3,2,1,0:T(8,128)(2,1)S(1)} custom-call(bf16[1,256,16384]{2,1,0:T(8,128)(2,1)} %vecs.1, f32[1,16384]{1,0:T(1,128)} %poles.1, f32[1,16384]{1,0:T(1,128)} %weights.1, s32[1,16384]{1,0:T(1,128)} %kept.1, f32[1,128]{1,0:T(1,128)} %bitcast.3, s32[1,512]{1,0:T(1,128)} %bitcast.2), custom_call_target="tpu_custom_call" | custom-call | tf_op jit(solution)/shard_map/merge/pallas_call | solution.py:218
  16.8 0.7 %copy.8 = bf16[1,4,2,32,256]{4,3,2,1,0:T(8,128)(2,1)} copy(bf16[1,4,2,32,256]{4,3,2,1,0:T(8,128)(2,1)S(1)} %merge.1) | data formatting | bytes 262144

commit v6 on v5

--- a/solution.py
+++ b/solution.py
@@ -197,7 +197,7 @@
             for h in range(n_half):
                 root_copy(o, h).wait_send()
 
-    for o in range(groups):
+    for o in range(groups - 1, -1, -1):
         g = lax.rem(me + groups - o, groups)
         piece = jnp.zeros((depth, share), jnp.float32)
         for t in [*range(1, n_col), 0]:

time: 17.8 us -> 17.9 us (level)
  the two profiles are of different devices: /device:TPU:0 before, /device:TPU:3 now
where the time goes in v6:
time: 17.9 us; the launch traced here: 17.7 us
  Pallas kernels  17.1 us (96%)
  local copies, waits for them, and re-layouts  0.66 us (4%)
    pallas_call x1, Pallas kernels, body(): pl.pallas_call(functools.partial(kernel, (n_row, n_col, n_half, cols, pan...  17.1 us
    unnamed x1, local copies, waits for them, and re-layouts  0.66 us

profile of v6, /device:TPU:3, one launch (start us, length us, event | category | flops | bytes accessed | tf_op | source)
XLA Modules:
  0.0 17.7 jit_solution(9083144725976966025)
XLA Ops:
  0.0 17.1 %merge.1 = bf16[1,4,2,32,256]{4,3,2,1,0:T(8,128)(2,1)S(1)} custom-call(bf16[1,256,16384]{2,1,0:T(8,128)(2,1)} %vecs.1, f32[1,16384]{1,0:T(1,128)} %poles.1, f32[1,16384]{1,0:T(1,128)} %weights.1, s32[1,16384]{1,0:T(1,128)} %kept.1, f32[1,128]{1,0:T(1,128)} %bitcast.3, s32[1,512]{1,0:T(1,128)} %bitcast.2), custom_call_target="tpu_custom_call" | custom-call | tf_op jit(solution)/shard_map/merge/pallas_call | solution.py:218
  17.1 0.7 %copy.8 = bf16[1,4,2,32,256]{4,3,2,1,0:T(8,128)(2,1)} copy(bf16[1,4,2,32,256]{4,3,2,1,0:T(8,128)(2,1)S(1)} %merge.1) | data formatting | bytes 262144
